TPU v7x, 128 devices: a whole 4x4x4 slice. The times are simulated.
128 devices in a mesh: clus: 8 (over x, core), trow: 4 (over y), tcol: 4 (over z).
Axes of the slice: x: 4, y: 4, z: 4, core: 2. Of those that a mesh axis runs over, the one named last changes fastest.
Arguments:
- embeddings: bfloat16 [65536, 1024], P(('clus', 'trow', 'tcol'))
- target: int32 [65536], P(('clus', 'trow', 'tcol')), may hold values from 0 to 98303, as said below
Outputs:
- best_cosine: float32 [65536], P(('clus', 'trow', 'tcol'))
Inputs may be any that keep to these rules, and one draw needn't show every extreme that they name: `target`: the grid has 8 clusters of 12288 slots each; the rows of a cluster fill its slots 0 to its size - 1, each slot once; every cluster has a row, and the last cluster is the largest and fills all 12288 slots. The rows of one device send at most 6 rows to any aligned block of 768 slots, and some block receives exactly 6 from every device.
All inputs are finite; a program needn't handle non-finite values.
Results may differ from a plain program's by a relative error of at most 0.00069.
Values may be sent and summed in bfloat16 or wider, within the bound.
A program may use at most 128 MiB of HBM per device.

v0:
```python
import jax
import jax.numpy as jnp
from jax import lax
from jax.sharding import PartitionSpec as P

SLOTS = 768
epsilon = 1e-06
ABSENT = 4.0


def on_device(embeddings, target):
    width = embeddings.shape[1]
    clusters_count = lax.axis_size("clus")
    tile_rows = lax.axis_size("trow")
    tile_cols = lax.axis_size("tcol")
    group_count = tile_rows * tile_cols
    devices = clusters_count * group_count
    pair_rows = SLOTS // devices
    values = embeddings.astype(jnp.float32)
    unit_rows = (
        values / jnp.sqrt(jnp.sum(values * values, axis=1, keepdims=True) + epsilon)
    ).astype(jnp.bfloat16)
    destination = target // SLOTS
    onehot = (destination[:, None] == jnp.arange(devices, dtype=jnp.int32)[None, :]).astype(
        jnp.int32
    )
    position = jnp.sum(onehot * (jnp.cumsum(onehot, axis=0) - 1), axis=1)
    buffer_slot = destination * pair_rows + position
    outgoing = jnp.full((SLOTS, width), ABSENT, jnp.bfloat16).at[buffer_slot].set(unit_rows)
    arrived = lax.all_to_all(
        outgoing.reshape(devices, pair_rows, width),
        ("clus", "trow", "tcol"),
        split_axis=0,
        concat_axis=0,
        tiled=True,
    ).reshape(SLOTS, width)
    row_pos = lax.axis_index("trow")
    col_pos = lax.axis_index("tcol")
    row_block = lax.all_gather(arrived, "tcol", axis=0, tiled=True)
    col_block = lax.all_gather(arrived, "trow", axis=0, tiled=True)
    local = jnp.arange(SLOTS, dtype=jnp.int32)
    row_index = (
        (row_pos * tile_cols + jnp.arange(tile_cols, dtype=jnp.int32))[:, None] * SLOTS
        + local[None, :]
    ).reshape(-1)
    col_index = (
        (jnp.arange(tile_rows, dtype=jnp.int32) * tile_cols + col_pos)[:, None] * SLOTS
        + local[None, :]
    ).reshape(-1)
    present = col_block[:, 0].astype(jnp.float32) < 2.0
    scores = lax.dot_general(
        row_block, col_block, (((1,), (1,)), ((), ())), preferred_element_type=jnp.float32
    )
    keep = present[None, :] & (col_index[None, :] != row_index[:, None])
    partial = jnp.max(jnp.where(keep, scores, -1.0), axis=1)
    outbound = partial.reshape(tile_cols, devices, pair_rows).transpose(1, 0, 2)
    returned = lax.all_to_all(
        outbound, ("clus", "trow", "tcol"), split_axis=0, concat_axis=0, tiled=True
    )
    best = jnp.max(
        returned.reshape(clusters_count, tile_rows, tile_cols, tile_cols, pair_rows), axis=2
    ).reshape(SLOTS)
    return best[buffer_slot]


def solution(mesh):
    in_specs = (P(("clus", "trow", "tcol"), None), P(("clus", "trow", "tcol")))
    out_specs = P(("clus", "trow", "tcol"))
    return jax.shard_map(
        on_device, mesh=mesh, in_specs=in_specs, out_specs=out_specs, check_vma=False
    )
```

profile of v0, /device:TPU:1, one launch (start us, length us, event | category | flops | bytes accessed | tf_op | source)
XLA Modules:
  0.0 249.8 jit_solution(1314348164494295271)
XLA Ops:
  6.5 0.0 all-gather.3.cloned.1.call-start
  6.5 0.7 fusion.14
  7.2 0.7 add_select_fusion
  7.9 0.1 copy.5
  8.0 0.2 fusion.8
  8.3 0.1 add_add_fusion
  8.4 0.2 fusion.7
  8.6 0.7 compare_select_fusion
  9.3 1.5 fusion
  10.8 4.6 %scatter_custom_fusion = bf16[768,1024]{1,0:T(8,128)(2,1)} fusion(s32[512]{0:T(512)S(1)} %compare_select_fusion, bf16[512,1024]{1,0:T(8,128)(2,1)} %param.2, f32[512]{0:T(512)S(1)} %add_sqrt_fusion, bf16[]{:T(256)} %constant.14.clone.1), kind=kCustom, calls=%fused_computation.9 | custom fusion | flops 1572864 | bytes 2623490 | tf_op jit(solution)/shard_map/scatter | solution.py:29
  15.4 2.5 reshape.90
  17.9 40.8 %all_to_all.10 = bf16[128,6,1024]{2,1,0:T(8,128)(2,1)} all-to-all(bf16[128,6,1024]{2,1,0:T(8,128)(2,1)S(1)} %reshape.90), channel_id=1, replica_groups=mesh['clus'=8,'trow'=4,'tcol'=4] {'clus','trow','tcol'}, dimensions={0} | all-to-all | bytes 3145728 | tf_op jit(solution)/shard_map/all_to_all | solution.py:30
  58.7 3.7 %reshape.91 = bf16[768,1024]{1,0:T(8,128)(2,1)} reshape(bf16[128,6,1024]{2,1,0:T(8,128)(2,1)} %all_to_all.10) | data formatting | bytes 3145728 | tf_op jit(solution)/shard_map/reshape | solution.py:36
  62.4 0.0 all-gather.3.cloned.1.call-update
  62.4 0.0 all-gather.5.cloned.1.call-start
  62.4 0.7 all-gather.5.cloned.1.call-update
  63.2 0.1 iota_add_fusion
  63.2 0.1 iota_add_fusion.1
  63.3 61.4 %all-gather.3.cloned.1.call-done = bf16[3072,1024]{1,0:T(8,128)(2,1)} async-done(((bf16[768,1024]{1,0:T(8,128)(2,1)}), bf16[3072,1024]{1,0:T(8,128)(2,1)}) %all-gather.3.cloned.1.call-update) | async-done | bytes 6291472 | tf_op jit(solution)/shard_map/all_gather | solution.py:40
  124.8 1.6 fusion.2
  126.4 66.6 %all-gather.5.cloned.1.call-done = bf16[3072,1024]{1,0:T(8,128)(2,1)} async-done(((bf16[768,1024]{1,0:T(8,128)(2,1)}), bf16[3072,1024]{1,0:T(8,128)(2,1)}) %all-gather.5.cloned.1.call-update) | async-done | bytes 6291472 | tf_op jit(solution)/shard_map/all_gather | solution.py:39
  193.0 25.1 %select_reduce_fusion = f32[3072]{0:T(1024)S(1)} fusion(bf16[3072,1024]{1,0:T(8,128)(2,1)} %all-gather.5.cloned.1.call-done, bf16[3072,1024]{1,0:T(8,128)(2,1)} %all-gather.3.cloned.1.call-done, s32[3072]{0:T(1024)S(1)} %add.97, s32[3072]{0:T(1024)S(1)} %add.91, pred[3072]{0:T(1024)(128)(4,1)S(1)} %fusion.2), kind=kOutput, calls=%fused_computation.2 | convolution fusion | flops 19365097472 | bytes 12622848 | tf_op jit(solution)/shard_map/dot_general | solution.py:51
  218.1 0.2 reshape.92
  218.3 0.9 copy.7
  219.2 8.9 %all-to-all-start.1 = ((f32[128,4,6]{2,1,0:T(4,128)}), f32[128,4,6]{2,1,0:T(4,128)S(1)}, u32[]{:S(2)}, u32[]{:S(2)}) async-start(f32[128,4,6]{2,1,0:T(4,128)} %copy.7), calls=%async_computation.1 | async-start | bytes 524288 | tf_op jit(solution)/shard_map/all_to_all | solution.py:57
  228.1 11.2 %all-to-all-done.1 = f32[128,4,6]{2,1,0:T(4,128)S(1)} async-done(((f32[128,4,6]{2,1,0:T(4,128)}), f32[128,4,6]{2,1,0:T(4,128)S(1)}, u32[]{:S(2)}, u32[]{:S(2)}) %all-to-all-start.1) | async-done | bytes 12320 | tf_op jit(solution)/shard_map/all_to_all | solution.py:57
  239.3 0.1 bitcast_reduce_fusion
  239.4 0.1 reshape.94
  239.5 3.4 %gather_fusion = f32[512]{0:T(512)} fusion(f32[768]{0:T(1024)S(1)} %reshape.94, s32[1024]{0:T(1024)S(1)} %pad_clamp_fusion), kind=kCustom, calls=%fused_computation | custom fusion | bytes 6144 | tf_op jit(solution)/shard_map/gather | solution.py:63
  (10 shorter events, 0.1 us)
Async XLA Ops:
  6.5 118.2 %all-gather.3.cloned.1.call-start = ((), (), s32[]{:S(2)}) async-start(), calls=%async_computation.2 | async-start | bytes 7864320 | tf_op jit(solution)/shard_map/all_gather | solution.py:40
  62.4 130.6 %all-gather.5.cloned.1.call-start = ((), (), s32[]{:S(2)}) async-start(), calls=%async_computation.3 | async-start | bytes 7864320 | tf_op jit(solution)/shard_map/all_gather | solution.py:39
  219.2 20.2 %all-to-all-start.1 = ((f32[128,4,6]{2,1,0:T(4,128)}), f32[128,4,6]{2,1,0:T(4,128)S(1)}, u32[]{:S(2)}, u32[]{:S(2)}) async-start(f32[128,4,6]{2,1,0:T(4,128)} %copy.7), calls=%async_computation.1 | async-start | bytes 524288 | tf_op jit(solution)/shard_map/all_to_all | solution.py:57
Sparse Core Ops, SparseCore 0:
  62.5 62.2 all-gather.2
  126.4 66.4 all-gather.4
where the time goes:
time: 250 us
  waiting for transfers between devices  140 us (56%)
  blocking collectives  40.8 us (16%)
  matrix products  25.1 us (10%)
  between operations  13.5 us (5%)
  local copies, waits for them, and re-layouts  11 us (4%)
  other arithmetic  10.6 us (4%)
  starting transfers between devices  8.98 us (4%)
    all_gather x1, waiting for transfers between devices, on_device(): row_block = lax.all_gather(arrived, 'tcol', axis=0, tiled=True)  66.6 us
    all_gather x1, waiting for transfers between devices, on_device(): col_block = lax.all_gather(arrived, 'trow', axis=0, tiled=True)  61.4 us
    all_to_all x1, blocking collectives, on_device(): lax.all_to_all(outgoing.reshape(devices, pair_rows, width), ('clus', 'tro...  40.8 us
    dot_general x1, matrix products, on_device(): lax.dot_general(row_block, col_block, (((1,), (1,)), ((), ())), preferred...  25.1 us
    all_to_all x1, waiting for transfers between devices, on_device(): lax.all_to_all(outbound, ('clus', 'trow', 'tcol'), split_axis=0, concat_a...  11.2 us
    all_to_all x1, starting transfers between devices, on_device(): lax.all_to_all(outbound, ('clus', 'trow', 'tcol'), split_axis=0, concat_a...  8.94 us
  transfers between devices with their start and end apart: 3, of which 3 were waited for; matrix products, arithmetic and copies ran while one was open for 1% of the time, Pallas kernels for 0%

commit v1 on v0

--- a/solution.py
+++ b/solution.py
@@ -6,6 +6,27 @@
 SLOTS = 768
 epsilon = 1e-06
 ABSENT = 4.0
+
+
+def collect(x, axis, dim):
+    size, mine, extent = (lax.axis_size(axis), lax.axis_index(axis), x.shape[dim])
+    right = [(i, (i + 1) % size) for i in range(size)]
+    downward = [(i, (i - 1) % size) for i in range(size)]
+    whole = jnp.zeros((*x.shape[:dim], size * extent, *x.shape[dim + 1 :]), x.dtype)
+    whole = lax.dynamic_update_slice_in_dim(whole, x, mine * extent, axis=dim)
+    from_left = from_right = x
+    halfway = size // 2
+    for step in range(1, halfway + 1):
+        from_left = lax.ppermute(from_left, axis, right)
+        whole = lax.dynamic_update_slice_in_dim(
+            whole, from_left, (mine - step) % size * extent, axis=dim
+        )
+        if step < size - halfway:
+            from_right = lax.ppermute(from_right, axis, downward)
+            whole = lax.dynamic_update_slice_in_dim(
+                whole, from_right, (mine + step) % size * extent, axis=dim
+            )
+    return whole
 
 
 def on_device(embeddings, target):
@@ -36,7 +57,7 @@
     ).reshape(SLOTS, width)
     row_pos = lax.axis_index("trow")
     col_pos = lax.axis_index("tcol")
-    row_block = lax.all_gather(arrived, "tcol", axis=0, tiled=True)
+    row_block = collect(arrived, "tcol", 0)
     col_block = lax.all_gather(arrived, "trow", axis=0, tiled=True)
     local = jnp.arange(SLOTS, dtype=jnp.int32)
     row_index = (

time: 250 us -> 195 us (0.78)
  waiting for transfers between devices: 140 us -> 70.6 us
  local copies, waits for them, and re-layouts: 11 us -> 22.4 us
  starting transfers between devices: 8.98 us -> 11.6 us
    all_gather x1 -> x0, waiting for transfers between devices: 66.6 us -> none  [on_device(): row_block = lax.all_gather(arrived, 'tcol', axis=0, tiled=True)]
    all_gather x1, waiting for transfers between devices: 61.4 us -> 0.01 us  [on_device(): col_block = lax.all_gather(arrived, 'trow', axis=0, tiled=True)]
    ppermute x0 -> x3, waiting for transfers between devices: none -> 59.4 us  [the longest x2 59.3 us: collect(): from_left = lax.ppermute(from_left, axis, right)]
    dynamic_update_slice x0 -> x4, local copies, waits for them, and re-layouts: none -> 8.01 us  [the longest x2 3.95 us: collect(): lax.dynamic_update_slice_in_dim(whole, from_left, (mine - step) % size *...]
    broadcast_in_dim x0 -> x1, local copies, waits for them, and re-layouts: none -> 3.46 us  [collect(): jnp.zeros((*x.shape[:dim], size * extent, *x.shape[dim + 1:]), x.dtype)]
    ppermute x0 -> x3, starting transfers between devices: none -> 2.75 us  [the longest x1 1.82 us: collect(): from_right = lax.ppermute(from_right, axis, downward)]
  transfers between devices with their start and end apart: 3 -> 5, of which waited for: 3 -> 3; matrix products, arithmetic and copies ran while one was open for 1% -> 6% of each run, Pallas kernels for 0% -> 0%
where the time goes in v1:
time: 195 us
  waiting for transfers between devices  70.6 us (36%)
  blocking collectives  40.8 us (21%)
  matrix products  25.1 us (13%)
  local copies, waits for them, and re-layouts  22.4 us (11%)
  between operations  13.5 us (7%)
  starting transfers between devices  11.6 us (6%)
  other arithmetic  10.6 us (5%)
    ppermute x2, waiting for transfers between devices, collect(): from_left = lax.ppermute(from_left, axis, right)  59.3 us
    all_to_all x1, blocking collectives, on_device(): lax.all_to_all(outgoing.reshape(devices, pair_rows, width), ('clus', 'tro...  40.8 us
    dot_general x1, matrix products, on_device(): lax.dot_general(row_block, col_block, (((1,), (1,)), ((), ())), preferred...  25.1 us
    all_to_all x1, waiting for transfers between devices, on_device(): lax.all_to_all(outbound, ('clus', 'trow', 'tcol'), split_axis=0, concat_a...  11.2 us
    all_to_all x1, starting transfers between devices, on_device(): lax.all_to_all(outbound, ('clus', 'trow', 'tcol'), split_axis=0, concat_a...  8.84 us
    scatter x1, other arithmetic, on_device(): jnp.full((SLOTS, width), ABSENT, jnp.bfloat16).at[buffer_slot]  4.59 us
    dynamic_update_slice x2, local copies, waits for them, and re-layouts, collect(): lax.dynamic_update_slice_in_dim(whole, from_left, (mine - step) % size *...  3.95 us
  transfers between devices with their start and end apart: 5, of which 3 were waited for; matrix products, arithmetic and copies ran while one was open for 6% of the time, Pallas kernels for 0%

profile of v1, /device:TPU:1, one launch (start us, length us, event | category | flops | bytes accessed | tf_op | source)
XLA Modules:
  0.0 194.5 jit_solution(5053925908349976161)
XLA Ops:
  6.5 0.7 fusion.14
  7.2 0.7 add_select_fusion
  7.9 0.1 copy.5
  8.0 0.2 fusion.8
  8.3 0.1 add_add_fusion
  8.4 0.2 fusion.7
  8.6 0.7 compare_select_fusion
  9.3 1.5 fusion
  10.8 4.6 %scatter_custom_fusion = bf16[768,1024]{1,0:T(8,128)(2,1)} fusion(s32[512]{0:T(512)S(1)} %compare_select_fusion, bf16[512,1024]{1,0:T(8,128)(2,1)} %param.2, f32[512]{0:T(512)S(1)} %add_sqrt_fusion, bf16[]{:T(256)} %constant.54.clone.1), kind=kCustom, calls=%fused_computation.9 | custom fusion | flops 1572864 | bytes 2623490 | tf_op jit(solution)/shard_map/scatter | solution.py:50
  15.4 2.5 %reshape.90 = bf16[128,6,1024]{2,1,0:T(8,128)(2,1)S(1)} reshape(bf16[768,1024]{1,0:T(8,128)(2,1)} %scatter_custom_fusion) | data formatting | bytes 3145728 | tf_op jit(solution)/shard_map/reshape | solution.py:52
  17.9 40.8 %all_to_all.10 = bf16[128,6,1024]{2,1,0:T(8,128)(2,1)} all-to-all(bf16[128,6,1024]{2,1,0:T(8,128)(2,1)S(1)} %reshape.90), channel_id=1, replica_groups=mesh['clus'=8,'trow'=4,'tcol'=4] {'clus','trow','tcol'}, dimensions={0} | all-to-all | bytes 3145728 | tf_op jit(solution)/shard_map/all_to_all | solution.py:51
  58.7 3.7 %reshape.91 = bf16[768,1024]{1,0:T(8,128)(2,1)} reshape(bf16[128,6,1024]{2,1,0:T(8,128)(2,1)} %all_to_all.10) | data formatting | bytes 3145728 | tf_op jit(solution)/shard_map/reshape | solution.py:57
  62.4 0.9 collective-permute-start
  63.3 1.8 collective-permute-start.1
  65.1 33.3 %collective-permute-done = bf16[768,1024]{1,0:T(8,128)(2,1)S(1)} collective-permute-done((bf16[768,1024]{1,0:T(8,128)(2,1)}, bf16[768,1024]{1,0:T(8,128)(2,1)S(1)}, u32[]{:S(2)}, u32[]{:S(2)}) %collective-permute-start) | collective-permute-done | bytes 1572896 | tf_op jit(solution)/shard_map/ppermute | solution.py:20
  98.5 0.1 iota_add_fusion.1
  98.6 0.1 iota_add_fusion
  98.7 3.5 %broadcast_in_dim.11 = bf16[3072,1024]{1,0:T(8,128)(2,1)} broadcast(bf16[]{:T(256)} %constant.66.clone.1), dimensions={} | broadcast | bytes 6291458 | tf_op jit(solution)/shard_map/broadcast_in_dim | solution.py:15
  102.1 1.3 constant_dynamic-update-slice_fusion.2
  103.4 1.3 constant_dynamic-update-slice_fusion.1
  104.6 2.8 %constant_dynamic-update-slice_fusion = bf16[3072,1024]{1,0:T(8,128)(2,1)} fusion(bf16[3072,1024]{1,0:T(8,128)(2,1)} %constant_dynamic-update-slice_fusion.1, bf16[768,1024]{1,0:T(8,128)(2,1)} %collective-permute-done.1, s32[]{:T(128)S(6)} %select_n.46), kind=kLoop, calls=%fused_computation.31 | loop fusion | bytes 3145732 | tf_op jit(solution)/shard_map/dynamic_update_slice | solution.py:26
  107.4 26.0 %collective-permute-done.2 = bf16[768,1024]{1,0:T(8,128)(2,1)} collective-permute-done((bf16[768,1024]{1,0:T(8,128)(2,1)S(1)}, bf16[768,1024]{1,0:T(8,128)(2,1)}, u32[]{:S(2)}, u32[]{:S(2)}) %collective-permute-start.2) | collective-permute-done | bytes 1572896 | tf_op jit(solution)/shard_map/ppermute | solution.py:20
  133.5 2.7 %constant_dynamic-update-slice_fusion.3 = bf16[3072,1024]{1,0:T(8,128)(2,1)} fusion(bf16[3072,1024]{1,0:T(8,128)(2,1)} %constant_dynamic-update-slice_fusion, bf16[768,1024]{1,0:T(8,128)(2,1)} %collective-permute-done.2, s32[]{:T(128)S(6)} %select_n.48), kind=kLoop, calls=%fused_computation.34 | loop fusion | bytes 3145732 | tf_op jit(solution)/shard_map/dynamic_update_slice | solution.py:21
  136.2 1.6 fusion.2
  137.8 25.1 %select_reduce_fusion = f32[3072]{0:T(1024)S(1)} fusion(bf16[3072,1024]{1,0:T(8,128)(2,1)} %constant_dynamic-update-slice_fusion.3, bf16[3072,1024]{1,0:T(8,128)(2,1)} %all-gather.2.cloned.1.call-done, s32[3072]{0:T(1024)S(1)} %add.124, s32[3072]{0:T(1024)S(1)} %add.118, pred[3072]{0:T(1024)(128)(4,1)S(1)} %fusion.2), kind=kOutput, calls=%fused_computation.2 | convolution fusion | flops 19365097472 | bytes 12622848 | tf_op jit(solution)/shard_map/dot_general | solution.py:72
  162.9 0.2 reshape.92
  163.1 0.9 copy.7
  164.0 8.8 %all-to-all-start.1 = ((f32[128,4,6]{2,1,0:T(4,128)}), f32[128,4,6]{2,1,0:T(4,128)S(1)}, u32[]{:S(2)}, u32[]{:S(2)}) async-start(f32[128,4,6]{2,1,0:T(4,128)} %copy.7), calls=%async_computation.1 | async-start | bytes 524288 | tf_op jit(solution)/shard_map/all_to_all | solution.py:78
  172.8 11.2 %all-to-all-done.1 = f32[128,4,6]{2,1,0:T(4,128)S(1)} async-done(((f32[128,4,6]{2,1,0:T(4,128)}), f32[128,4,6]{2,1,0:T(4,128)S(1)}, u32[]{:S(2)}, u32[]{:S(2)}) %all-to-all-start.1) | async-done | bytes 12320 | tf_op jit(solution)/shard_map/all_to_all | solution.py:78
  184.1 0.1 bitcast_reduce_fusion
  184.1 0.1 reshape.94
  184.3 3.4 %gather_fusion = f32[512]{0:T(512)} fusion(f32[768]{0:T(1024)S(1)} %reshape.94, s32[1024]{0:T(1024)S(1)} %pad_clamp_fusion), kind=kCustom, calls=%fused_computation | custom fusion | bytes 6144 | tf_op jit(solution)/shard_map/gather | solution.py:84
  (17 shorter events, 0.1 us)
Async XLA Ops:
  6.5 129.6 %all-gather.2.cloned.1.call-start = ((), (), s32[]{:S(2)}) async-start(), calls=%async_computation.2 | async-start | bytes 7864320 | tf_op jit(solution)/shard_map/all_gather | solution.py:61
  62.4 39.8 %copy-start = (bf16[768,1024]{1,0:T(8,128)(2,1)S(1)}, bf16[768,1024]{1,0:T(8,128)(2,1)}, u32[]{:S(2)}) copy-start(bf16[768,1024]{1,0:T(8,128)(2,1)} %reshape.91) | copy-start | bytes 4718596
  62.4 36.1 %collective-permute-start = (bf16[768,1024]{1,0:T(8,128)(2,1)}, bf16[768,1024]{1,0:T(8,128)(2,1)S(1)}, u32[]{:S(2)}, u32[]{:S(2)}) collective-permute-start(bf16[768,1024]{1,0:T(8,128)(2,1)} %reshape.91), channel_id=1, source_target_pairs={{0,1},{1,2},{2,3},{3,0},{4,5},{5,6},{6,7},{7,4},{8,9},{9,10},{10,1... | collective-permute-start | bytes 4718600 | tf_op jit(solution)/shard_map/ppermute | solution.py:20
  63.3 41.3 %collective-permute-start.1 = (bf16[768,1024]{1,0:T(8,128)(2,1)}, bf16[768,1024]{1,0:T(8,128)(2,1)}, u32[]{:S(2)}, u32[]{:S(2)}) collective-permute-start(bf16[768,1024]{1,0:T(8,128)(2,1)} %reshape.91), channel_id=1, source_target_pairs={{0,3},{1,0},{2,1},{3,2},{4,7},{5,4},{6,5},{7,6},{8,11},{9,8},{10,9... | collective-permute-start | bytes 4718600 | tf_op jit(solution)/shard_map/ppermute | solution.py:25
  98.4 35.0 %collective-permute-start.2 = (bf16[768,1024]{1,0:T(8,128)(2,1)S(1)}, bf16[768,1024]{1,0:T(8,128)(2,1)}, u32[]{:S(2)}, u32[]{:S(2)}) collective-permute-start(bf16[768,1024]{1,0:T(8,128)(2,1)S(1)} %collective-permute-done), channel_id=1, source_target_pairs={{0,1},{1,2},{2,3},{3,0},{4,5},{5,6},{6,7},{7,4},{8,9},{9,10},{10,1... | collective-permute-start | bytes 4718600 | tf_op jit(solution)/shard_map/ppermute | solution.py:20
  164.0 20.1 %all-to-all-start.1 = ((f32[128,4,6]{2,1,0:T(4,128)}), f32[128,4,6]{2,1,0:T(4,128)S(1)}, u32[]{:S(2)}, u32[]{:S(2)}) async-start(f32[128,4,6]{2,1,0:T(4,128)} %copy.7), calls=%async_computation.1 | async-start | bytes 524288 | tf_op jit(solution)/shard_map/all_to_all | solution.py:78
Sparse Core Ops, SparseCore 0:
  62.5 62.2 all-gather.1
